TPU v7x, 32 devices: a whole 2x2x4 slice. The times are simulated.
32 devices in a mesh: fsdp: 2 (over x), ctx: 4 (over y, core), tp: 4 (over z).
Axes of the slice: x: 2, y: 2, z: 4, core: 2. Of those that a mesh axis runs over, the one named last changes fastest.
Arguments:
- block_in: bfloat16 [8, 1024, 2048], P('fsdp', 'ctx', 'tp'), may hold values from -6 to 6
- seg_ids: int32 [8, 1024], P('fsdp'), may hold values from 0 to 7, never falling along the last dimension, each value on 1 to 512 neighbouring positions
- out_cot: bfloat16 [8, 1024, 2048], P('fsdp', 'ctx'), may hold values from -6 to 6
- norm_gain: bfloat16 [2048], P('tp'), may hold values from 0.099609375 to 1.8984375
- mid_gain: bfloat16 [2048], P('tp'), may hold values from 0.099609375 to 1.8984375
- gelu_proj: bfloat16 [2048, 2816], P(('fsdp', 'ctx'), 'tp'), may hold values from -0.125 to 0.125
- scan_proj: bfloat16 [2048, 2816], P(('fsdp', 'ctx'), 'tp'), may hold values from -0.125 to 0.125
- out_proj: bfloat16 [2816, 2048], P('tp', ('fsdp', 'ctx')), may hold values from -0.4375 to 0.4375
- gate_proj: bfloat16 [2048, 6144], P(('fsdp', 'ctx'), 'tp'), may hold values from -0.125 to 0.125
- up_proj: bfloat16 [2048, 6144], P(('fsdp', 'ctx'), 'tp'), may hold values from -0.125 to 0.125
- down_proj: bfloat16 [6144, 2048], P('tp', ('fsdp', 'ctx')), may hold values from -0.109375 to 0.109375
- conv_kernel: float32 [4, 2816], P(None, 'tp'), may hold values from -3 to 3
- conv_bias: float32 [2816], P('tp'), may hold values from -3 to 3
- rate_gate: bfloat16 [16, 176, 176], P('tp'), may hold values from -0.4375 to 0.4375
- input_gate: bfloat16 [16, 176, 176], P('tp'), may hold values from -0.4375 to 0.4375
- rate_bias: float32 [2816], P('tp'), may hold values from -4 to 4
- input_bias: float32 [2816], P('tp'), may hold values from -4 to 4
- decay_param: float32 [2816], P('tp'), may hold values from -16 to -4
Outputs:
- block_out: bfloat16 [8, 1024, 2048], P('fsdp', 'ctx', 'tp')
- grad_in: float32 [8, 1024, 2048], P('fsdp', 'ctx', 'tp')
- grad_norm_gain: float32 [2048], P('tp')
- grad_mid_gain: float32 [2048], P('tp')
- grad_gelu_proj: float32 [2048, 2816], P(('fsdp', 'ctx'), 'tp')
- grad_scan_proj: float32 [2048, 2816], P(('fsdp', 'ctx'), 'tp')
- grad_out_proj: float32 [2816, 2048], P('tp', ('fsdp', 'ctx'))
- grad_gate_proj: float32 [2048, 6144], P(('fsdp', 'ctx'), 'tp')
- grad_up_proj: float32 [2048, 6144], P(('fsdp', 'ctx'), 'tp')
- grad_down_proj: float32 [6144, 2048], P('tp', ('fsdp', 'ctx'))
- grad_conv_kernel: float32 [4, 2816], P(None, 'tp')
- grad_conv_bias: float32 [2816], P('tp')
- grad_rate_gate: float32 [16, 176, 176], P('tp')
- grad_input_gate: float32 [16, 176, 176], P('tp')
- grad_rate_bias: float32 [2816], P('tp')
- grad_input_bias: float32 [2816], P('tp')
- grad_decay_param: float32 [2816], P('tp')
Inputs may be any that keep to these rules, and one draw needn't show every extreme that they name: `seg_ids`: in every row the document numbers never fall; each of the 8 documents covers 1 to 512 positions, and one covers exactly 512.
All inputs are finite; a program needn't handle non-finite values.
Results may differ from a plain program's by a relative error of at most 0.0095.
Values may be sent and summed in bfloat16 or wider, within the bound.
A program may use at most 320 MiB of HBM per device.

v0:
```python
import jax
import jax.numpy as jnp
from jax import lax
from jax.sharding import PartitionSpec as P

CONV = 4
eps_norm = 1e-06


def from_behind(value, axis, steps):
    count = lax.axis_size(axis)
    leading, last = (max(0, -steps), min(count, count - steps))
    return lax.ppermute(value, axis, [(source, source + steps) for source in range(leading, last)])


def entering(value, axis, join, neutral, backward):
    count, mine = (lax.axis_size(axis), lax.axis_index(axis))
    pieces = jax.tree.map(lambda part: lax.all_gather(part, axis), value)
    if backward:
        pieces = jax.tree.map(lambda part: part[::-1], pieces)
        mine = count - 1 - mine
    total = jax.tree.map(
        lambda part, zero: jnp.full_like(part, 0) + jnp.asarray(zero, part.dtype), value, neutral
    )

    def step(position, total):
        longer = join(total, jax.tree.map(lambda part: part[position], pieces))
        return jax.tree.map(lambda new, old: jnp.where(position < mine, new, old), longer, total)

    return lax.fori_loop(0, count - 1, step, total)


def rms_scale(values, gain_vec):
    return (
        values * lax.rsqrt(jnp.mean(values * values, axis=-1, keepdims=True) + eps_norm) * gain_vec
    )


def gelu_tanh(values):
    return jax.nn.gelu(values, approximate=True)


def gate_values(pre_rate, pre_input, decay_param):
    rate_vals = jax.nn.sigmoid(pre_rate)
    input_vals = jax.nn.sigmoid(pre_input)
    log_a = -8.0 * jax.nn.softplus(decay_param) * rate_vals
    return (jnp.exp(log_a), jnp.sqrt(-jnp.expm1(2.0 * log_a)) * input_vals)


def combine(first_part, second_part):
    return (first_part[0] * second_part[0], second_part[0] * first_part[1] + second_part[1])


def matmul(left, right):
    return jnp.dot(left, right, preferred_element_type=jnp.float32)


def matmul_rt(left, right):
    return lax.dot_general(
        left, right, (((1,), (1,)), ((), ())), preferred_element_type=jnp.float32
    )


def matmul_lt(left, right):
    return lax.dot_general(
        left, right, (((0,), (0,)), ((), ())), preferred_element_type=jnp.float32
    )


def shards(
    block_in,
    seg_ids,
    out_cot,
    norm_gain,
    mid_gain,
    gelu_proj,
    scan_proj,
    out_proj,
    gate_proj,
    up_proj,
    down_proj,
    conv_kernel,
    conv_bias,
    rate_gate,
    input_gate,
    rate_bias,
    input_bias,
    decay_param,
):
    seq_count, tok_count, part_width = block_in.shape
    row_count = seq_count * tok_count
    full_in, gain_one, gain_two = (
        lax.all_gather(block_in, "tp", axis=2, tiled=True),
        lax.all_gather(norm_gain, "tp", axis=0, tiled=True),
        lax.all_gather(mid_gain, "tp", axis=0, tiled=True),
    )
    w_gelu, w_scan, w_out, w_gate, w_up, w_down = (
        lax.all_gather(gelu_proj, ("fsdp", "ctx"), axis=0, tiled=True),
        lax.all_gather(scan_proj, ("fsdp", "ctx"), axis=0, tiled=True),
        lax.all_gather(out_proj, ("fsdp", "ctx"), axis=1, tiled=True),
        lax.all_gather(gate_proj, ("fsdp", "ctx"), axis=0, tiled=True),
        lax.all_gather(up_proj, ("fsdp", "ctx"), axis=0, tiled=True),
        lax.all_gather(down_proj, ("fsdp", "ctx"), axis=1, tiled=True),
    )
    full_width = full_in.shape[2]
    rec_width = w_gelu.shape[1]
    head_count = rate_gate.shape[0]
    head_size = rate_gate.shape[1]
    x_rows = full_in.reshape(row_count, full_width).astype(jnp.float32)
    normed_f, norm_one_back = jax.vjp(rms_scale, x_rows, gain_one.astype(jnp.float32))
    normed = normed_f.astype(jnp.bfloat16)
    y_pre = matmul(normed, w_gelu)
    y_act, y_back = jax.vjp(gelu_tanh, y_pre)
    x_branch = matmul(normed, w_scan).astype(jnp.bfloat16).reshape(seq_count, tok_count, rec_width)
    margin_len = CONV - 1
    start_tok = lax.axis_index("ctx") * tok_count
    padded_ids = jnp.concatenate(
        [
            jnp.full((seq_count, margin_len), -1, jnp.int32),
            seg_ids,
            jnp.full((seq_count, margin_len), -2, jnp.int32),
        ],
        axis=1,
    )
    window_ids = lax.dynamic_slice_in_dim(padded_ids, start_tok, tok_count + 2 * margin_len, 1)
    own_ids = window_ids[:, margin_len : margin_len + tok_count]
    back_masks = [
        (window_ids[:, margin_len - offset : margin_len - offset + tok_count] == own_ids).astype(
            jnp.float32
        )[..., None]
        for offset in range(CONV)
    ]
    ahead_masks = [
        (window_ids[:, margin_len + offset : margin_len + offset + tok_count] == own_ids).astype(
            jnp.float32
        )[..., None]
        for offset in range(CONV)
    ]
    prev_edge = from_behind(x_branch[:, tok_count - margin_len :, :], "ctx", 1)
    ext_x = jnp.concatenate([prev_edge, x_branch], axis=1)
    conv_sum = conv_bias + jnp.zeros((seq_count, tok_count, rec_width), jnp.float32)
    for offset in range(CONV):
        conv_sum = (
            conv_sum
            + conv_kernel[offset]
            * ext_x[:, margin_len - offset : margin_len - offset + tok_count].astype(jnp.float32)
            * back_masks[offset]
        )
    conv_out = conv_sum.astype(jnp.bfloat16)
    conv_vals = conv_out.astype(jnp.float32)
    heads_in = conv_out.reshape(row_count, head_count, head_size)
    pre_rate = (
        jnp.einsum("rhi,hij->rhj", heads_in, rate_gate, preferred_element_type=jnp.float32).reshape(
            row_count, rec_width
        )
        + rate_bias
    )
    pre_input = (
        jnp.einsum(
            "rhi,hij->rhj", heads_in, input_gate, preferred_element_type=jnp.float32
        ).reshape(row_count, rec_width)
        + input_bias
    )
    (decays, in_scale), gate_back = jax.vjp(gate_values, pre_rate, pre_input, decay_param)
    in_scale3 = in_scale.reshape(seq_count, tok_count, rec_width)
    coeffs = decays.reshape(seq_count, tok_count, rec_width) * back_masks[1]
    inputs = in_scale3 * conv_vals
    cum_coef, local_state = lax.associative_scan(combine, (coeffs, inputs), axis=1)
    ones_row = jnp.ones((seq_count, rec_width), jnp.float32)
    zeros_row = jnp.zeros((seq_count, rec_width), jnp.float32)
    _, state_in = entering(
        (cum_coef[:, -1], local_state[:, -1]), "ctx", combine, (ones_row, zeros_row), False
    )
    states = local_state + cum_coef * state_in[:, None, :]
    state_rows = states.reshape(row_count, rec_width)
    mixed_in = (state_rows * y_act).astype(jnp.bfloat16)
    rec_part = matmul(mixed_in, w_out)
    col_start = lax.axis_index("tp") * part_width
    rec_total = lax.psum(rec_part, "tp")
    mid_rows = x_rows + rec_total
    normed_mid_f, norm_two_back = jax.vjp(rms_scale, mid_rows, gain_two.astype(jnp.float32))
    normed_mid = normed_mid_f.astype(jnp.bfloat16)
    gate_pre = matmul(normed_mid, w_gate)
    up_pre = matmul(normed_mid, w_up)
    gate_act, gate_act_back = jax.vjp(gelu_tanh, gate_pre)
    hidden = (gate_act * up_pre).astype(jnp.bfloat16)
    mlp_slice = lax.psum_scatter(matmul(hidden, w_down), "tp", scatter_dimension=1, tiled=True)
    mid_own = lax.dynamic_slice_in_dim(mid_rows, col_start, part_width, 1)
    block_out = (mid_own + mlp_slice).astype(jnp.bfloat16).reshape(seq_count, tok_count, part_width)
    cot_rows = out_cot.reshape(row_count, full_width)
    hid_grad = matmul_rt(cot_rows, w_down)
    grad_down = matmul_lt(hidden, cot_rows)
    gate_grad = gate_act_back(hid_grad * up_pre)[0].astype(jnp.bfloat16)
    up_grad = (hid_grad * gate_act).astype(jnp.bfloat16)
    grad_gate = matmul_lt(normed_mid, gate_grad)
    grad_up = matmul_lt(normed_mid, up_grad)
    mid_part = matmul_rt(gate_grad, w_gate) + matmul_rt(up_grad, w_up)
    mid_norm_grad = lax.psum(mid_part, "tp")
    mid_from_norm, gain_two_grad = norm_two_back(mid_norm_grad)
    mid_grad = cot_rows.astype(jnp.float32) + mid_from_norm
    rec_grad = mid_grad.astype(jnp.bfloat16)
    mixed_grad = matmul_rt(rec_grad, w_out)
    grad_out = matmul_lt(mixed_in, rec_grad)
    state_direct = (mixed_grad * y_act).reshape(seq_count, tok_count, rec_width)
    y_grad = y_back(mixed_grad * state_rows)[0].astype(jnp.bfloat16)
    grad_gelu = matmul_lt(normed, y_grad)
    in_part = matmul_rt(y_grad, w_gelu)
    next_coef = jnp.concatenate(
        [coeffs[:, 1:], jnp.ones((seq_count, 1, rec_width), jnp.float32)], axis=1
    )
    tail_coef, local_grad = lax.associative_scan(
        combine, (next_coef, state_direct), reverse=True, axis=1
    )
    head_coef = coeffs[:, 0]
    _, grad_in_state = entering(
        (head_coef * tail_coef[:, 0], head_coef * local_grad[:, 0]),
        "ctx",
        combine,
        (ones_row, zeros_row),
        True,
    )
    state_grad = local_grad + tail_coef * grad_in_state[:, None, :]
    prev_states = jnp.concatenate([state_in[:, None, :], states[:, :-1]], axis=1)
    decay_grad = (state_grad * prev_states * back_masks[1]).reshape(row_count, rec_width)
    scale_grad = (state_grad * conv_vals).reshape(row_count, rec_width)
    conv_direct = (state_grad * in_scale3).reshape(row_count, rec_width)
    rate_raw, input_raw, grad_decay = gate_back((decay_grad, scale_grad))
    rate_grad = rate_raw.astype(jnp.bfloat16)
    input_grad = input_raw.astype(jnp.bfloat16)
    rate_heads = rate_grad.reshape(row_count, head_count, head_size)
    input_heads = input_grad.reshape(row_count, head_count, head_size)
    grad_rate_gate = jnp.einsum(
        "rhi,rhj->hij", heads_in, rate_heads, preferred_element_type=jnp.float32
    )
    grad_input_gate = jnp.einsum(
        "rhi,rhj->hij", heads_in, input_heads, preferred_element_type=jnp.float32
    )
    grad_rate_bias = jnp.sum(rate_grad.astype(jnp.float32), axis=0)
    grad_input_bias = jnp.sum(input_grad.astype(jnp.float32), axis=0)
    gate_back_in = jnp.einsum(
        "rhj,hij->rhi", rate_heads, rate_gate, preferred_element_type=jnp.float32
    ) + jnp.einsum("rhj,hij->rhi", input_heads, input_gate, preferred_element_type=jnp.float32)
    conv_grad = (
        (conv_direct + gate_back_in.reshape(row_count, rec_width))
        .astype(jnp.bfloat16)
        .reshape(seq_count, tok_count, rec_width)
    )
    next_edge = from_behind(conv_grad[:, :margin_len, :], "ctx", -1)
    ext_grad = jnp.concatenate([conv_grad, next_edge], axis=1)
    conv_grad_f = conv_grad.astype(jnp.float32)
    branch_grad = jnp.zeros((seq_count, tok_count, rec_width), jnp.float32)
    kernel_rows = []
    for offset in range(CONV):
        branch_grad = (
            branch_grad
            + conv_kernel[offset]
            * ext_grad[:, offset : offset + tok_count].astype(jnp.float32)
            * ahead_masks[offset]
        )
        kernel_rows.append(
            jnp.sum(
                conv_grad_f
                * ext_x[:, margin_len - offset : margin_len - offset + tok_count].astype(
                    jnp.float32
                )
                * back_masks[offset],
                axis=(0, 1),
            )
        )
    grad_kernel = jnp.stack(kernel_rows)
    grad_conv = jnp.sum(conv_grad_f, axis=(0, 1))
    branch_low = branch_grad.astype(jnp.bfloat16).reshape(row_count, rec_width)
    grad_scan = matmul_lt(normed, branch_low)
    in_part = in_part + matmul_rt(branch_low, w_scan)
    in_from_norm, gain_one_part = norm_one_back(in_part)
    in_slice, gain_one_slice = (
        lax.psum_scatter(in_from_norm, "tp", scatter_dimension=1, tiled=True),
        lax.psum_scatter(gain_one_part, "tp", scatter_dimension=0, tiled=True),
    )
    grad_in = (lax.dynamic_slice_in_dim(mid_grad, col_start, part_width, 1) + in_slice).reshape(
        seq_count, tok_count, part_width
    )
    gain_two_slice = lax.dynamic_slice_in_dim(gain_two_grad, col_start, part_width, 0)
    grad_gelu_s, grad_scan_s, grad_out_s, grad_gate_s, grad_up_s, grad_down_s = (
        lax.psum_scatter(grad_gelu, ("fsdp", "ctx"), scatter_dimension=0, tiled=True),
        lax.psum_scatter(grad_scan, ("fsdp", "ctx"), scatter_dimension=0, tiled=True),
        lax.psum_scatter(grad_out, ("fsdp", "ctx"), scatter_dimension=1, tiled=True),
        lax.psum_scatter(grad_gate, ("fsdp", "ctx"), scatter_dimension=0, tiled=True),
        lax.psum_scatter(grad_up, ("fsdp", "ctx"), scatter_dimension=0, tiled=True),
        lax.psum_scatter(grad_down, ("fsdp", "ctx"), scatter_dimension=1, tiled=True),
    )
    (
        gain_one_total,
        gain_two_total,
        kernel_total,
        conv_total,
        rate_gate_total,
        input_gate_total,
        rate_bias_total,
        input_bias_total,
        decay_total,
    ) = lax.psum(
        (
            gain_one_slice,
            gain_two_slice,
            grad_kernel,
            grad_conv,
            grad_rate_gate,
            grad_input_gate,
            grad_rate_bias,
            grad_input_bias,
            grad_decay,
        ),
        ("fsdp", "ctx"),
    )
    return (
        block_out,
        grad_in,
        gain_one_total,
        gain_two_total,
        grad_gelu_s,
        grad_scan_s,
        grad_out_s,
        grad_gate_s,
        grad_up_s,
        grad_down_s,
        kernel_total,
        conv_total,
        rate_gate_total,
        input_gate_total,
        rate_bias_total,
        input_bias_total,
        decay_total,
    )


def solution(mesh):
    in_specs = (
        P("fsdp", "ctx", "tp"),
        P("fsdp", None),
        P("fsdp", "ctx", None),
        P("tp"),
        P("tp"),
        P(("fsdp", "ctx"), "tp"),
        P(("fsdp", "ctx"), "tp"),
        P("tp", ("fsdp", "ctx")),
        P(("fsdp", "ctx"), "tp"),
        P(("fsdp", "ctx"), "tp"),
        P("tp", ("fsdp", "ctx")),
        P(None, "tp"),
        P("tp"),
        P("tp", None, None),
        P("tp", None, None),
        P("tp"),
        P("tp"),
        P("tp"),
    )
    out_specs = (
        P("fsdp", "ctx", "tp"),
        P("fsdp", "ctx", "tp"),
        P("tp"),
        P("tp"),
        P(("fsdp", "ctx"), "tp"),
        P(("fsdp", "ctx"), "tp"),
        P("tp", ("fsdp", "ctx")),
        P(("fsdp", "ctx"), "tp"),
        P(("fsdp", "ctx"), "tp"),
        P("tp", ("fsdp", "ctx")),
        P(None, "tp"),
        P("tp"),
        P("tp", None, None),
        P("tp", None, None),
        P("tp"),
        P("tp"),
        P("tp"),
    )
    return jax.shard_map(shards, mesh=mesh, in_specs=in_specs, out_specs=out_specs, check_vma=False)
```

profile of v0, /device:TPU:0, one launch (start us, length us, event | category | flops | bytes accessed | tf_op | source)
XLA Modules:
  0.0 2524.0 jit_solution(14394685174451569282)
XLA Ops:
  10.7 13.5 all-gather.4
  26.8 66.3 %all-gather.14.cloned.1.call-done = bf16[4,256,2048]{2,1,0:T(8,128)(2,1)} async-done(((bf16[4,256,512]{2,1,0:T(8,128)(2,1)}), bf16[4,256,2048]{2,1,0:T(8,128)(2,1)}) %all-gather.14.cloned.1.call-update) | async-done | bytes 4194320 | tf_op jit(solution)/shard_map/all_gather | solution.py:93
  100.0 25.2 all-gather.16.cloned.1.call-done
  179.3 10.2 slice.580
  189.5 9.6 slice.581
  374.8 9.6 slice.635
  527.0 9.7 multiply_convert_fusion.3
  547.9 12.2 all-gather.5
  560.1 277.4 %all-reduce.73.cloned.1.call-done = f32[1024,2048]{1,0:T(8,128)} async-done(((f32[1024,2048]{1,0:T(8,128)}), f32[1024,2048]{1,0:T(8,128)}) %all-reduce.73.cloned.1.call-update) | async-done | bytes 8388624 | tf_op jit(solution)/shard_map/psum | solution.py:179
  849.7 34.1 %all-gather.22.cloned.1.call-done = bf16[2048,1536]{1,0:T(8,128)(2,1)} async-done(((bf16[256,1536]{1,0:T(8,128)(2,1)}), bf16[2048,1536]{1,0:T(8,128)(2,1)}) %all-gather.22.cloned.1.call-update) | async-done | bytes 6291472 | tf_op jit(solution)/shard_map/all_gather | solution.py:101
  883.8 11.8 fusion.117
  895.7 35.6 %all-gather.24.cloned.1.call-done = bf16[2048,1536]{1,0:T(8,128)(2,1)} async-done(((bf16[256,1536]{1,0:T(8,128)(2,1)}), bf16[2048,1536]{1,0:T(8,128)(2,1)}) %all-gather.24.cloned.1.call-update) | async-done | bytes 6291472 | tf_op jit(solution)/shard_map/all_gather | solution.py:102
  931.3 11.9 fusion.118
  943.1 36.7 %all-gather.26.cloned.1.call-done = bf16[1536,2048]{1,0:T(8,128)(2,1)} async-done(((bf16[1536,256]{1,0:T(8,128)(2,1)}), bf16[1536,2048]{1,0:T(8,128)(2,1)}) %all-gather.26.cloned.1.call-update) | async-done | bytes 6291472 | tf_op jit(solution)/shard_map/all_gather | solution.py:103
  979.9 18.6 multiply_convert_fusion.1
  998.4 10.0 fusion.120
  1008.5 10.9 convolution_add_fusion.1
  1023.8 9.7 slice.657
  1033.4 9.6 slice.664
  1043.0 9.5 slice.655
  1053.1 12.8 slice.658
  1065.9 12.7 slice.665
  1078.7 12.8 slice.656
  1091.5 11.9 fusion.119
  1103.5 206.9 %all-reduce.75.cloned.1.call-done = f32[1024,2048]{1,0:T(8,128)} async-done(((f32[1024,2048]{1,0:T(8,128)}), f32[1024,2048]{1,0:T(8,128)}) %all-reduce.75.cloned.1.call-update) | async-done | bytes 8388624 | tf_op jit(solution)/shard_map/psum | solution.py:198
  1325.5 11.8 fusion.72
  1340.8 9.5 slice.659
  1350.4 9.6 slice.661
  1359.9 12.8 slice.660
  1372.7 12.8 slice.662
  1480.8 9.5 slice.717
  1641.5 12.8 slice.718
  1695.7 24.7 rev.15
  1720.5 24.8 rev.14
  1747.6 11.8 multiply_reduce_fusion.3
  1799.5 10.8 fusion.43
  1859.0 12.5 fusion.122
  1871.8 12.6 fusion.123
  1884.4 12.2 fusion.124
  1908.5 26.4 %all-reduce.67 = (f32[512]{0:T(512)}, f32[512]{0:T(512)}, f32[4,704]{1,0:T(4,128)}, f32[704]{0:T(1024)}, f32[704]{0:T(1024)}, /*index=5*/f32[704]{0:T(1024)}, f32[704]{0:T(1024)}) all-reduce(f32[512]{0:T(512)S(1)} %dynamic-slice.3, f32[512]{0:T(512)S(1)} %dynamic_slice.43, ...), channel_id=1, replica_groups=mesh['fsdp'=2,'ctx'=4,'tp'=4] {'fsdp','ctx'}, use_global_device_ids=true, to_apply=%region_14.15 | all-reduce | flops 6656 | bytes 53248 | tf_op jit(solution)/shard_map/psum | solution.py:302
  1938.5 33.6 %reduce-scatter.11.cloned.1.call-done = f32[1024,512]{1,0:T(8,128)} async-done(((f32[1024,2048]{1,0:T(8,128)}), f32[1024,512]{1,0:T(8,128)}) %reduce-scatter.11.cloned.1.call-update) | async-done | bytes 2097168 | tf_op jit(solution)/shard_map/reduce_scatter | solution.py:277
  1976.2 58.8 %all-reduce.77.cloned.1.call-done = (f32[4,176,176]{2,1,0:T(8,128)}, f32[4,176,176]{2,1,0:T(8,128)}) async-done(((f32[4,176,176]{2,1,0:T(8,128)}, f32[4,176,176]{2,1,0:T(8,128)}), (f32[4,176,176]{2,1,0:T(8,128)}, f32[4,176,176]{2,1,0:T(8,128)})) %all-reduce.77.cloned.1.call-update) | async-done | bytes 991248 | tf_op jit(solution)/shard_map/psum | solution.py:302
  2034.9 62.7 %reduce-scatter.17.cloned.1.call-done = f32[704,256]{1,0:T(8,128)} async-done(((f32[704,2048]{1,0:T(8,128)}), f32[704,256]{1,0:T(8,128)}) %reduce-scatter.17.cloned.1.call-update) | async-done | bytes 720912 | tf_op jit(solution)/shard_map/reduce_scatter | solution.py:287
  2097.6 63.0 %reduce-scatter.13.cloned.1.call-done = f32[256,704]{0,1:T(8,128)} async-done(((f32[2048,704]{0,1:T(8,128)}), f32[256,704]{0,1:T(8,128)}) %reduce-scatter.13.cloned.1.call-update) | async-done | bytes 720912 | tf_op jit(solution)/shard_map/reduce_scatter | solution.py:285
  2160.6 63.3 %reduce-scatter.15.cloned.1.call-done = f32[256,704]{0,1:T(8,128)} async-done(((f32[2048,704]{0,1:T(8,128)}), f32[256,704]{0,1:T(8,128)}) %reduce-scatter.15.cloned.1.call-update) | async-done | bytes 720912 | tf_op jit(solution)/shard_map/reduce_scatter | solution.py:286
  2223.9 96.3 %reduce-scatter.19.cloned.1.call-done = f32[256,1536]{1,0:T(8,128)} async-done(((f32[2048,1536]{1,0:T(8,128)}), f32[256,1536]{1,0:T(8,128)}) %reduce-scatter.19.cloned.1.call-update) | async-done | bytes 1572880 | tf_op jit(solution)/shard_map/reduce_scatter | solution.py:288
  2320.2 96.3 %reduce-scatter.21.cloned.1.call-done = f32[256,1536]{1,0:T(8,128)} async-done(((f32[2048,1536]{1,0:T(8,128)}), f32[256,1536]{1,0:T(8,128)}) %reduce-scatter.21.cloned.1.call-update) | async-done | bytes 1572880 | tf_op jit(solution)/shard_map/reduce_scatter | solution.py:289
  2416.5 96.4 %reduce-scatter.23.cloned.1.call-done = f32[1536,256]{1,0:T(8,128)} async-done(((f32[1536,2048]{1,0:T(8,128)}), f32[1536,256]{1,0:T(8,128)}) %reduce-scatter.23.cloned.1.call-update) | async-done | bytes 1572880 | tf_op jit(solution)/shard_map/reduce_scatter | solution.py:290
  (615 shorter events, 837.6 us)
Async XLA Ops:
  7.2 141.0 %copy-start = (bf16[4,176,176]{2,1,0:T(8,128)(2,1)S(1)}, bf16[4,176,176]{2,1,0:T(8,128)(2,1)}, u32[]{:S(2)}) copy-start(bf16[4,176,176]{2,1,0:T(8,128)(2,1)} %param.35) | copy-start | bytes 743428
  7.2 85.9 %all-gather.14.cloned.1.call-start = ((), (), s32[]{:S(2)}) async-start(), calls=%async_computation.8 | async-start | bytes 5242880 | tf_op jit(solution)/shard_map/all_gather | solution.py:93
  7.9 117.3 %all-gather.16.cloned.1.call-start = ((), (), s32[]{:S(2)}) async-start(), calls=%async_computation.9 | async-start | bytes 3244032 | tf_op jit(solution)/shard_map/all_gather | solution.py:99
  8.7 518.3 %all-gather.18.cloned.1.call-start = ((), (), s32[]{:S(2)}) async-start(), calls=%async_computation.10 | async-start | bytes 3244032 | tf_op jit(solution)/shard_map/all_gather | solution.py:98
  9.4 527.2 %all-gather.20.cloned.1.call-start = ((), (), s32[]{:S(2)}) async-start(), calls=%async_computation.11 | async-start | bytes 3244032 | tf_op jit(solution)/shard_map/all_gather | solution.py:100
  10.0 827.5 %all-reduce.73.cloned.1.call-start = ((), (), s32[]{:S(2)}) async-start(), calls=%async_computation.12 | async-start | bytes 16777216 | tf_op jit(solution)/shard_map/psum | solution.py:179
  24.3 75.8 %copy-start.51 = (f32[4,1,512]{2,1,0:T(1,128)}, f32[4,1,512]{2,1,0:T(1,128)S(1)}, u32[]{:S(2)}) copy-start(f32[4,1,512]{2,1,0:T(1,128)S(1)} %convert_element_type.180) | copy-start | bytes 24580
  25.2 113.3 %copy-start.71 = (f32[704]{0:T(1024)}, f32[704]{0:T(1024)S(1)}, u32[]{:S(2)}) copy-start(f32[704]{0:T(1024)S(1)} %get-tuple-element.255) | copy-start | bytes 8452
  25.2 113.3 %copy-start.73 = (f32[704]{0:T(1024)}, f32[704]{0:T(1024)S(1)}, u32[]{:S(2)}) copy-start(f32[704]{0:T(1024)S(1)} %get-tuple-element.256) | copy-start | bytes 8452
  25.2 113.3 %copy-start.75 = (f32[704]{0:T(1024)}, f32[704]{0:T(1024)S(1)}, u32[]{:S(2)}) copy-start(f32[704]{0:T(1024)S(1)} %get-tuple-element.257) | copy-start | bytes 8452
  25.2 113.3 %copy-start.77 = (f32[704]{0:T(1024)}, f32[704]{0:T(1024)S(1)}, u32[]{:S(2)}) copy-start(f32[704]{0:T(1024)S(1)} %get-tuple-element.258) | copy-start | bytes 8452
  25.9 993.5 %copy-start.49 = (f32[704]{0:T(1024)}, f32[704]{0:T(1024)S(1)}, u32[]{:S(2)}) copy-start(f32[704]{0:T(1024)S(1)} %fusion.94) | copy-start | bytes 8452
  134.1 4.3 collective-permute-start
  137.2 35.1 %copy-start.47 = (f32[4,256]{1,0:T(4,128)}, f32[4,256]{1,0:T(4,128)S(1)}, u32[]{:S(2)}) copy-start(f32[4,256]{1,0:T(4,128)S(1)} %get-tuple-element.377) | copy-start | bytes 12292
  158.1 14.2 copy-start.4
  179.3 19.8 copy-start.6
  301.5 37.3 %copy-start.67 = (f32[4,1,704]{2,1,0:T(1,128)S(1)}, f32[4,1,704]{2,1,0:T(1,128)}, u32[]{:S(2)}) copy-start(f32[4,1,704]{2,1,0:T(1,128)} %slice.752) | copy-start | bytes 33796
  545.8 338.1 %all-gather.22.cloned.1.call-start = ((), (), s32[]{:S(2)}) async-start(), calls=%async_computation.13 | async-start | bytes 7077888 | tf_op jit(solution)/shard_map/all_gather | solution.py:101
  546.4 384.9 %all-gather.24.cloned.1.call-start = ((), (), s32[]{:S(2)}) async-start(), calls=%async_computation.14 | async-start | bytes 7077888 | tf_op jit(solution)/shard_map/all_gather | solution.py:102
  547.1 432.8 %all-gather.26.cloned.1.call-start = ((), (), s32[]{:S(2)}) async-start(), calls=%async_computation.15 | async-start | bytes 7077888 | tf_op jit(solution)/shard_map/all_gather | solution.py:103
  547.9 762.5 %all-reduce.75.cloned.1.call-start = ((), (), s32[]{:S(2)}) async-start(), calls=%async_computation.17 | async-start | bytes 16777216 | tf_op jit(solution)/shard_map/psum | solution.py:198
  560.1 750.3 %copy-start.42 = (f32[4,1,512]{2,1,0:T(1,128)}, f32[4,1,512]{2,1,0:T(1,128)S(1)}, u32[]{:S(2)}) copy-start(f32[4,1,512]{2,1,0:T(1,128)S(1)} %convert_element_type.181) | copy-start | bytes 24580
  843.4 467.0 %copy-start.53 = (f32[1024]{0:T(1024)}, f32[1024]{0:T(1024)S(1)}, u32[]{:S(2)}) copy-start(f32[1024]{0:T(1024)S(1)} %fusion.101) | copy-start | bytes 12292
  1019.4 915.5 %reduce-scatter.9.cloned.1.call-start = ((), (), s32[]{:S(2)}) async-start(), calls=%async_computation.16 | async-start | bytes 10485760 | tf_op jit(solution)/shard_map/reduce_scatter | solution.py:187
  1103.4 868.7 %reduce-scatter.11.cloned.1.call-start = ((), (), s32[]{:S(2)}) async-start(), calls=%async_computation.18 | async-start | bytes 10485760 | tf_op jit(solution)/shard_map/reduce_scatter | solution.py:277
  1325.5 11.8 copy-start.15
  1523.2 30.4 %copy-start.66 = (f32[4,1,704]{2,1,0:T(1,128)S(1)}, f32[4,1,704]{2,1,0:T(1,128)}, u32[]{:S(2)}) copy-start(f32[4,1,704]{2,1,0:T(1,128)} %slice.804) | copy-start | bytes 33796
  1531.5 30.1 %copy-start.65 = (f32[4,1,704]{2,1,0:T(1,128)S(1)}, f32[4,1,704]{2,1,0:T(1,128)}, u32[]{:S(2)}) copy-start(f32[4,1,704]{2,1,0:T(1,128)} %slice.829) | copy-start | bytes 33796
  1574.4 15.6 copy-start.68
  1720.4 24.9 copy-start.39
  1720.4 27.1 %copy-start.5 = (f32[4,256,704]{2,1,0:T(8,128)S(1)}, f32[4,256,704]{2,1,0:T(8,128)}, u32[]{:S(2)}) copy-start(f32[4,256,704]{2,1,0:T(8,128)} %copy-done.4) | copy-start | bytes 8650756
  1720.4 27.1 %copy-start.48 = (f32[4,256]{1,0:T(4,128)S(1)}, f32[4,256]{1,0:T(4,128)}, u32[]{:S(2)}) copy-start(f32[4,256]{1,0:T(4,128)} %copy-done.47) | copy-start | bytes 12292
  1720.4 27.2 %copy-start.50 = (f32[704]{0:T(1024)S(1)}, f32[704]{0:T(1024)}, u32[]{:S(2)}) copy-start(f32[704]{0:T(1024)} %copy-done.49) | copy-start | bytes 8452
  1720.4 27.2 %copy-start.56 = (f32[704]{0:T(1024)S(1)}, f32[704]{0:T(1024)}, u32[]{:S(2)}) copy-start(f32[704]{0:T(1024)} %param.38) | copy-start | bytes 8452
  1720.5 27.2 %copy-start.59 = (f32[704]{0:T(1024)S(1)}, f32[704]{0:T(1024)}, u32[]{:S(2)}) copy-start(f32[704]{0:T(1024)} %param.37) | copy-start | bytes 8452
  1720.5 27.2 %copy-start.60 = (f32[4,1,704]{2,1,0:T(1,128)S(1)}, f32[4,1,704]{2,1,0:T(1,128)}, u32[]{:S(2)}) copy-start(f32[4,1,704]{2,1,0:T(1,128)} %broadcast_in_dim.10) | copy-start | bytes 33796
  1799.4 12.1 copy-start.107
  1799.5 12.1 copy-start.110
  1810.3 5.0 collective-permute-start.1
  1826.9 208.0 %all-reduce.77.cloned.1.call-start = ((), (), s32[]{:S(2)}) async-start(), calls=%async_computation.25 | async-start | bytes 2883584 | tf_op jit(solution)/shard_map/psum | solution.py:302
  1831.7 265.9 %reduce-scatter.17.cloned.1.call-start = ((), (), s32[]{:S(2)}) async-start(), calls=%async_computation.21 | async-start | bytes 6488064 | tf_op jit(solution)/shard_map/reduce_scatter | solution.py:287
  1840.8 319.8 %reduce-scatter.13.cloned.1.call-start = ((), (), s32[]{:S(2)}) async-start(), calls=%async_computation.19 | async-start | bytes 6488064 | tf_op jit(solution)/shard_map/reduce_scatter | solution.py:285
  1849.5 374.4 %reduce-scatter.15.cloned.1.call-start = ((), (), s32[]{:S(2)}) async-start(), calls=%async_computation.20 | async-start | bytes 6488064 | tf_op jit(solution)/shard_map/reduce_scatter | solution.py:286
  1858.9 461.3 %reduce-scatter.19.cloned.1.call-start = ((), (), s32[]{:S(2)}) async-start(), calls=%async_computation.22 | async-start | bytes 14155776 | tf_op jit(solution)/shard_map/reduce_scatter | solution.py:288
  1871.5 545.0 %reduce-scatter.21.cloned.1.call-start = ((), (), s32[]{:S(2)}) async-start(), calls=%async_computation.23 | async-start | bytes 14155776 | tf_op jit(solution)/shard_map/reduce_scatter | solution.py:289
  1884.3 628.6 %reduce-scatter.23.cloned.1.call-start = ((), (), s32[]{:S(2)}) async-start(), calls=%async_computation.24 | async-start | bytes 14155776 | tf_op jit(solution)/shard_map/reduce_scatter | solution.py:290
  1896.7 11.8 copy-start.95
  1896.7 11.8 copy-start.96
  (85 other events, 342.4 us)
Sparse Core Ops, SparseCore 0:
  9.6 83.4 all-gather.13
  95.0 30.1 all-gather.15
  127.1 31.8 all-gather.17
  160.7 31.6 all-gather.19
  545.9 291.5 all-reduce.72
  839.3 44.5 all-gather.21
  885.7 45.5 all-gather.23
  933.2 46.6 all-gather.25
  1019.5 290.8 all-reduce.74
  1312.6 143.4 reduce-scatter.8
  1827.0 145.0 reduce-scatter.10
  1975.8 59.0 all-reduce.76
  2039.3 58.2 reduce-scatter.16
  2101.5 59.0 reduce-scatter.12
  2164.8 58.9 reduce-scatter.14
  2227.8 92.3 reduce-scatter.18
  2324.1 92.3 reduce-scatter.20
  2420.5 92.3 reduce-scatter.22
where the time goes:
time: 2550 us; the launch traced here: 2520 us
  waiting for transfers between devices  1260 us (49%)
  local copies, waits for them, and re-layouts  706 us (28%)
  other arithmetic  262 us (10%)
  matrix products  194 us (8%)
  blocking collectives  83 us (3%)
    psum x1, waiting for transfers between devices, shards(): rec_total = lax.psum(rec_part, 'tp')  277 us
    slice x57, local copies, waits for them, and re-layouts, shards(): lax.associative_scan(combine, (next_coef, state_direct), reverse=True, ax...  215 us
    psum x1, waiting for transfers between devices, shards(): mid_norm_grad = lax.psum(mid_part, 'tp')  207 us
    slice x52, local copies, waits for them, and re-layouts, shards(): lax.associative_scan(combine, (coeffs, inputs), axis=1)  128 us
    pad x28, local copies, waits for them, and re-layouts, shards(): lax.associative_scan(combine, (coeffs, inputs), axis=1)  110 us
    pad x28, local copies, waits for them, and re-layouts, shards(): lax.associative_scan(combine, (next_coef, state_direct), reverse=True, ax...  108 us
    reduce_scatter x1, waiting for transfers between devices, shards(): lax.psum_scatter(grad_down, ('fsdp', 'ctx'), scatter_dimension=1, tiled=T...  96.4 us
    reduce_scatter x1, waiting for transfers between devices, shards(): lax.psum_scatter(grad_up, ('fsdp', 'ctx'), scatter_dimension=0, tiled=True)  96.3 us
  transfers between devices with their start and end apart: 20, of which 15 were waited for; matrix products, arithmetic and copies ran while one was open for 43% of the time, Pallas kernels for 0%

commit v1 on v0

--- a/solution.py
+++ b/solution.py
@@ -2,6 +2,7 @@
 import jax.numpy as jnp
 from jax import lax
 from jax.sharding import PartitionSpec as P
+from jax.lax import all_gather
 
 CONV = 4
 eps_norm = 1e-06
@@ -176,7 +177,7 @@
     mixed_in = (state_rows * y_act).astype(jnp.bfloat16)
     rec_part = matmul(mixed_in, w_out)
     col_start = lax.axis_index("tp") * part_width
-    rec_total = lax.psum(rec_part, "tp")
+    rec_total = jnp.sum(all_gather(rec_part, axis_name="tp"), axis=0)
     mid_rows = x_rows + rec_total
     normed_mid_f, norm_two_back = jax.vjp(rms_scale, mid_rows, gain_two.astype(jnp.float32))
     normed_mid = normed_mid_f.astype(jnp.bfloat16)

time: 2550 us -> 2830 us (1.11)
  waiting for transfers between devices: 1260 us -> 1510 us
    all_gather x0 -> x1, waiting for transfers between devices: none -> 548 us  [shards(): rec_total = jnp.sum(all_gather(rec_part, axis_name='tp'), axis=0)]
    psum x1 -> x0, waiting for transfers between devices: 277 us -> none  [shards(): rec_total = lax.psum(rec_part, 'tp')]
  transfers between devices with their start and end apart: 20 -> 20, of which waited for: 15 -> 15; matrix products, arithmetic and copies ran while one was open for 43% -> 40% of each run, Pallas kernels for 0% -> 0%
where the time goes in v1:
time: 2830 us; the launch traced here: 2800 us
  waiting for transfers between devices  1510 us (53%)
  local copies, waits for them, and re-layouts  710 us (25%)
  other arithmetic  284 us (10%)
  matrix products  192 us (7%)
  blocking collectives  83.2 us (3%)
    all_gather x1, waiting for transfers between devices, shards(): rec_total = jnp.sum(all_gather(rec_part, axis_name='tp'), axis=0)  548 us
    slice x57, local copies, waits for them, and re-layouts, shards(): lax.associative_scan(combine, (next_coef, state_direct), reverse=True, ax...  216 us
    psum x1, waiting for transfers between devices, shards(): mid_norm_grad = lax.psum(mid_part, 'tp')  207 us
    slice x52, local copies, waits for them, and re-layouts, shards(): lax.associative_scan(combine, (coeffs, inputs), axis=1)  127 us
    pad x28, local copies, waits for them, and re-layouts, shards(): lax.associative_scan(combine, (next_coef, state_direct), reverse=True, ax...  111 us
    pad x28, local copies, waits for them, and re-layouts, shards(): lax.associative_scan(combine, (coeffs, inputs), axis=1)  110 us
    reduce_scatter x1, waiting for transfers between devices, shards(): lax.psum_scatter(grad_down, ('fsdp', 'ctx'), scatter_dimension=1, tiled=T...  96.4 us
    reduce_scatter x1, waiting for transfers between devices, shards(): lax.psum_scatter(grad_up, ('fsdp', 'ctx'), scatter_dimension=0, tiled=True)  96.3 us
  transfers between devices with their start and end apart: 20, of which 15 were waited for; matrix products, arithmetic and copies ran while one was open for 40% of the time, Pallas kernels for 0%

profile of v1, /device:TPU:0, one launch (start us, length us, event | category | flops | bytes accessed | tf_op | source)
XLA Modules:
  0.0 2798.3 jit_solution(9545518365970534735)
XLA Ops:
  10.7 13.5 all-gather.5
  26.8 66.3 %all-gather.16.cloned.1.call-done = bf16[4,256,2048]{2,1,0:T(8,128)(2,1)} async-done(((bf16[4,256,512]{2,1,0:T(8,128)(2,1)}), bf16[4,256,2048]{2,1,0:T(8,128)(2,1)}) %all-gather.16.cloned.1.call-update) | async-done | bytes 4194320 | tf_op jit(solution)/shard_map/all_gather | solution.py:94
  100.0 25.2 all-gather.18.cloned.1.call-done
  179.1 10.1 slice.580
  189.2 9.5 slice.581
  373.5 9.6 slice.635
  525.9 9.6 multiply_convert_fusion.3
  546.8 11.9 all-gather.6
  558.7 548.1 %all-gather.30.cloned.1.call-done = f32[4096,2048]{1,0:T(8,128)} async-done(((f32[1024,2048]{1,0:T(8,128)}), f32[4096,2048]{1,0:T(8,128)}) %all-gather.30.cloned.1.call-update) | async-done | bytes 33554448 | tf_op jit(solution)/shard_map/all_gather | solution.py:180
  1106.9 16.9 reduce_sum.135
  1138.2 14.1 all-gather.24.cloned.1.call-done
  1152.3 11.7 fusion.118
  1164.1 35.7 %all-gather.26.cloned.1.call-done = bf16[2048,1536]{1,0:T(8,128)(2,1)} async-done(((bf16[256,1536]{1,0:T(8,128)(2,1)}), bf16[2048,1536]{1,0:T(8,128)(2,1)}) %all-gather.26.cloned.1.call-update) | async-done | bytes 6291472 | tf_op jit(solution)/shard_map/all_gather | solution.py:103
  1199.8 11.7 fusion.119
  1211.5 36.9 %all-gather.28.cloned.1.call-done = bf16[1536,2048]{1,0:T(8,128)(2,1)} async-done(((bf16[1536,256]{1,0:T(8,128)(2,1)}), bf16[1536,2048]{1,0:T(8,128)(2,1)}) %all-gather.28.cloned.1.call-update) | async-done | bytes 6291472 | tf_op jit(solution)/shard_map/all_gather | solution.py:104
  1248.4 18.8 multiply_convert_fusion.1
  1267.2 10.0 fusion.121
  1277.2 10.5 convolution_add_fusion.1
  1292.6 9.6 slice.657
  1302.3 9.5 slice.664
  1311.8 9.5 slice.655
  1322.0 12.8 slice.658
  1334.8 12.7 slice.665
  1347.5 12.8 slice.656
  1360.3 11.7 fusion.120
  1372.1 206.6 %all-reduce.72.cloned.1.call-done = f32[1024,2048]{1,0:T(8,128)} async-done(((f32[1024,2048]{1,0:T(8,128)}), f32[1024,2048]{1,0:T(8,128)}) %all-reduce.72.cloned.1.call-update) | async-done | bytes 8388624 | tf_op jit(solution)/shard_map/psum | solution.py:199
  1596.6 10.4 fusion.74
  1610.5 9.5 slice.659
  1620.0 9.6 slice.661
  1629.6 12.8 slice.660
  1642.4 12.9 slice.662
  1916.4 12.9 slice.718
  1970.6 24.7 rev.15
  1995.3 24.9 rev.14
  2022.6 11.9 multiply_reduce_fusion.2
  2074.1 10.9 fusion.45
  2133.4 12.5 fusion.123
  2146.2 12.6 fusion.124
  2158.9 12.3 fusion.125
  2183.1 26.4 all-reduce.67
  2213.1 33.4 %reduce-scatter.11.cloned.1.call-done = f32[1024,512]{1,0:T(8,128)} async-done(((f32[1024,2048]{1,0:T(8,128)}), f32[1024,512]{1,0:T(8,128)}) %reduce-scatter.11.cloned.1.call-update) | async-done | bytes 2097168 | tf_op jit(solution)/shard_map/reduce_scatter | solution.py:278
  2250.5 58.8 %all-reduce.74.cloned.1.call-done = (f32[4,176,176]{2,1,0:T(8,128)}, f32[4,176,176]{2,1,0:T(8,128)}) async-done(((f32[4,176,176]{2,1,0:T(8,128)}, f32[4,176,176]{2,1,0:T(8,128)}), (f32[4,176,176]{2,1,0:T(8,128)}, f32[4,176,176]{2,1,0:T(8,128)})) %all-reduce.74.cloned.1.call-update) | async-done | bytes 991248 | tf_op jit(solution)/shard_map/psum | solution.py:303
  2309.3 62.7 %reduce-scatter.17.cloned.1.call-done = f32[704,256]{1,0:T(8,128)} async-done(((f32[704,2048]{1,0:T(8,128)}), f32[704,256]{1,0:T(8,128)}) %reduce-scatter.17.cloned.1.call-update) | async-done | bytes 720912 | tf_op jit(solution)/shard_map/reduce_scatter | solution.py:288
  2371.9 63.0 %reduce-scatter.13.cloned.1.call-done = f32[256,704]{0,1:T(8,128)} async-done(((f32[2048,704]{0,1:T(8,128)}), f32[256,704]{0,1:T(8,128)}) %reduce-scatter.13.cloned.1.call-update) | async-done | bytes 720912 | tf_op jit(solution)/shard_map/reduce_scatter | solution.py:286
  2434.9 63.3 %reduce-scatter.15.cloned.1.call-done = f32[256,704]{0,1:T(8,128)} async-done(((f32[2048,704]{0,1:T(8,128)}), f32[256,704]{0,1:T(8,128)}) %reduce-scatter.15.cloned.1.call-update) | async-done | bytes 720912 | tf_op jit(solution)/shard_map/reduce_scatter | solution.py:287
  2498.2 96.3 %reduce-scatter.19.cloned.1.call-done = f32[256,1536]{1,0:T(8,128)} async-done(((f32[2048,1536]{1,0:T(8,128)}), f32[256,1536]{1,0:T(8,128)}) %reduce-scatter.19.cloned.1.call-update) | async-done | bytes 1572880 | tf_op jit(solution)/shard_map/reduce_scatter | solution.py:289
  2594.5 96.3 %reduce-scatter.21.cloned.1.call-done = f32[256,1536]{1,0:T(8,128)} async-done(((f32[2048,1536]{1,0:T(8,128)}), f32[256,1536]{1,0:T(8,128)}) %reduce-scatter.21.cloned.1.call-update) | async-done | bytes 1572880 | tf_op jit(solution)/shard_map/reduce_scatter | solution.py:290
  2690.9 96.4 %reduce-scatter.23.cloned.1.call-done = f32[1536,256]{1,0:T(8,128)} async-done(((f32[1536,2048]{1,0:T(8,128)}), f32[1536,256]{1,0:T(8,128)}) %reduce-scatter.23.cloned.1.call-update) | async-done | bytes 1572880 | tf_op jit(solution)/shard_map/reduce_scatter | solution.py:291
  (619 shorter events, 856.0 us)
Async XLA Ops:
  7.2 140.6 %copy-start = (bf16[4,176,176]{2,1,0:T(8,128)(2,1)S(1)}, bf16[4,176,176]{2,1,0:T(8,128)(2,1)}, u32[]{:S(2)}) copy-start(bf16[4,176,176]{2,1,0:T(8,128)(2,1)} %param.35) | copy-start | bytes 743428
  7.2 85.9 %all-gather.16.cloned.1.call-start = ((), (), s32[]{:S(2)}) async-start(), calls=%async_computation.8 | async-start | bytes 5242880 | tf_op jit(solution)/shard_map/all_gather | solution.py:94
  7.9 117.3 %all-gather.18.cloned.1.call-start = ((), (), s32[]{:S(2)}) async-start(), calls=%async_computation.9 | async-start | bytes 3244032 | tf_op jit(solution)/shard_map/all_gather | solution.py:100
  8.7 517.2 %all-gather.20.cloned.1.call-start = ((), (), s32[]{:S(2)}) async-start(), calls=%async_computation.10 | async-start | bytes 3244032 | tf_op jit(solution)/shard_map/all_gather | solution.py:99
  9.4 526.1 %all-gather.22.cloned.1.call-start = ((), (), s32[]{:S(2)}) async-start(), calls=%async_computation.11 | async-start | bytes 3244032 | tf_op jit(solution)/shard_map/all_gather | solution.py:101
  10.0 1096.9 %all-gather.30.cloned.1.call-start = ((), (), s32[]{:S(2)}) async-start(), calls=%async_computation.24 | async-start | bytes 41943040 | tf_op jit(solution)/shard_map/all_gather | solution.py:180
  24.3 75.7 %copy-start.46 = (f32[4,1,512]{2,1,0:T(1,128)}, f32[4,1,512]{2,1,0:T(1,128)S(1)}, u32[]{:S(2)}) copy-start(f32[4,1,512]{2,1,0:T(1,128)S(1)} %convert_element_type.181) | copy-start | bytes 24580
  25.2 113.3 %copy-start.66 = (f32[704]{0:T(1024)}, f32[704]{0:T(1024)S(1)}, u32[]{:S(2)}) copy-start(f32[704]{0:T(1024)S(1)} %get-tuple-element.255) | copy-start | bytes 8452
  25.2 113.3 %copy-start.68 = (f32[704]{0:T(1024)}, f32[704]{0:T(1024)S(1)}, u32[]{:S(2)}) copy-start(f32[704]{0:T(1024)S(1)} %get-tuple-element.256) | copy-start | bytes 8452
  25.2 113.3 %copy-start.70 = (f32[704]{0:T(1024)}, f32[704]{0:T(1024)S(1)}, u32[]{:S(2)}) copy-start(f32[704]{0:T(1024)S(1)} %get-tuple-element.257) | copy-start | bytes 8452
  25.2 113.3 %copy-start.72 = (f32[704]{0:T(1024)}, f32[704]{0:T(1024)S(1)}, u32[]{:S(2)}) copy-start(f32[704]{0:T(1024)S(1)} %get-tuple-element.258) | copy-start | bytes 8452
  25.9 146.1 %copy-start.43 = (f32[704]{0:T(1024)}, f32[704]{0:T(1024)S(1)}, u32[]{:S(2)}) copy-start(f32[704]{0:T(1024)S(1)} %fusion.96) | copy-start | bytes 8452
  134.1 4.3 collective-permute-start
  137.2 34.9 %copy-start.41 = (f32[4,256]{1,0:T(4,128)}, f32[4,256]{1,0:T(4,128)S(1)}, u32[]{:S(2)}) copy-start(f32[4,256]{1,0:T(4,128)S(1)} %get-tuple-element.377) | copy-start | bytes 12292
  157.8 14.2 copy-start.5
  179.1 19.6 copy-start.7
  296.0 42.3 %copy-start.62 = (f32[4,1,704]{2,1,0:T(1,128)S(1)}, f32[4,1,704]{2,1,0:T(1,128)}, u32[]{:S(2)}) copy-start(f32[4,1,704]{2,1,0:T(1,128)} %slice.752) | copy-start | bytes 33796
  544.6 607.7 %all-gather.24.cloned.1.call-start = ((), (), s32[]{:S(2)}) async-start(), calls=%async_computation.12 | async-start | bytes 7077888 | tf_op jit(solution)/shard_map/all_gather | solution.py:102
  545.2 654.6 %all-gather.26.cloned.1.call-start = ((), (), s32[]{:S(2)}) async-start(), calls=%async_computation.13 | async-start | bytes 7077888 | tf_op jit(solution)/shard_map/all_gather | solution.py:103
  546.0 702.4 %all-gather.28.cloned.1.call-start = ((), (), s32[]{:S(2)}) async-start(), calls=%async_computation.14 | async-start | bytes 7077888 | tf_op jit(solution)/shard_map/all_gather | solution.py:104
  546.7 1032.0 %all-reduce.72.cloned.1.call-start = ((), (), s32[]{:S(2)}) async-start(), calls=%async_computation.16 | async-start | bytes 16777216 | tf_op jit(solution)/shard_map/psum | solution.py:199
  1267.2 10.0 copy-start.102
  1287.7 921.7 %reduce-scatter.9.cloned.1.call-start = ((), (), s32[]{:S(2)}) async-start(), calls=%async_computation.15 | async-start | bytes 10485760 | tf_op jit(solution)/shard_map/reduce_scatter | solution.py:188
  1372.0 874.4 %reduce-scatter.11.cloned.1.call-start = ((), (), s32[]{:S(2)}) async-start(), calls=%async_computation.17 | async-start | bytes 10485760 | tf_op jit(solution)/shard_map/reduce_scatter | solution.py:278
  1578.7 11.5 copy-start.10
  1780.9 37.1 %copy-start.61 = (f32[4,1,704]{2,1,0:T(1,128)S(1)}, f32[4,1,704]{2,1,0:T(1,128)}, u32[]{:S(2)}) copy-start(f32[4,1,704]{2,1,0:T(1,128)} %slice.830) | copy-start | bytes 33796
  1790.0 38.4 %copy-start.60 = (f32[4,1,704]{2,1,0:T(1,128)S(1)}, f32[4,1,704]{2,1,0:T(1,128)}, u32[]{:S(2)}) copy-start(f32[4,1,704]{2,1,0:T(1,128)} %slice.804) | copy-start | bytes 33796
  1806.3 30.1 %copy-start.59 = (f32[4,1,704]{2,1,0:T(1,128)S(1)}, f32[4,1,704]{2,1,0:T(1,128)}, u32[]{:S(2)}) copy-start(f32[4,1,704]{2,1,0:T(1,128)} %slice.829) | copy-start | bytes 33796
  1849.2 15.5 copy-start.63
  1995.3 27.3 copy-start.6
  1995.3 27.3 copy-start.42
  1995.3 27.3 copy-start.45
  1995.3 27.3 copy-start.50
  1995.3 27.3 copy-start.53
  1995.3 27.3 copy-start.54
  2074.1 12.2 copy-start.104
  2074.1 12.2 copy-start.108
  2085.0 5.0 collective-permute-start.1
  2101.5 207.7 %all-reduce.74.cloned.1.call-start = ((), (), s32[]{:S(2)}) async-start(), calls=%async_computation.25 | async-start | bytes 2883584 | tf_op jit(solution)/shard_map/psum | solution.py:303
  2106.3 265.6 %reduce-scatter.17.cloned.1.call-start = ((), (), s32[]{:S(2)}) async-start(), calls=%async_computation.20 | async-start | bytes 6488064 | tf_op jit(solution)/shard_map/reduce_scatter | solution.py:288
  2115.4 319.5 %reduce-scatter.13.cloned.1.call-start = ((), (), s32[]{:S(2)}) async-start(), calls=%async_computation.18 | async-start | bytes 6488064 | tf_op jit(solution)/shard_map/reduce_scatter | solution.py:286
  2123.9 374.3 %reduce-scatter.15.cloned.1.call-start = ((), (), s32[]{:S(2)}) async-start(), calls=%async_computation.19 | async-start | bytes 6488064 | tf_op jit(solution)/shard_map/reduce_scatter | solution.py:287
  2133.4 461.1 %reduce-scatter.19.cloned.1.call-start = ((), (), s32[]{:S(2)}) async-start(), calls=%async_computation.21 | async-start | bytes 14155776 | tf_op jit(solution)/shard_map/reduce_scatter | solution.py:289
  2145.9 544.9 %reduce-scatter.21.cloned.1.call-start = ((), (), s32[]{:S(2)}) async-start(), calls=%async_computation.22 | async-start | bytes 14155776 | tf_op jit(solution)/shard_map/reduce_scatter | solution.py:290
  2158.8 628.4 %reduce-scatter.23.cloned.1.call-start = ((), (), s32[]{:S(2)}) async-start(), calls=%async_computation.23 | async-start | bytes 14155776 | tf_op jit(solution)/shard_map/reduce_scatter | solution.py:291
  2171.2 11.9 copy-start.92
  2171.2 11.9 copy-start.93
  2171.2 11.8 copy-start.94
  (85 other events, 348.9 us)
Sparse Core Ops, SparseCore 0:
  9.6 83.4 all-gather.15
  95.0 30.1 all-gather.17
  127.1 31.8 all-gather.19
  160.7 31.6 all-gather.21
  544.8 562.0 all-gather.29
  1108.6 43.6 all-gather.23
  1154.2 45.5 all-gather.25
  1201.7 46.6 all-gather.27
  1287.9 290.8 all-reduce.71
  1580.9 143.4 reduce-scatter.8
  2101.6 144.7 reduce-scatter.10
  2250.1 59.0 all-reduce.73
  2313.7 58.2 reduce-scatter.16
  2375.8 59.0 reduce-scatter.12
  2439.1 58.9 reduce-scatter.14
  2502.1 92.3 reduce-scatter.18
  2598.4 92.3 reduce-scatter.20
  2694.8 92.3 reduce-scatter.22
